TPU v7x, 256 devices: a whole 4x4x8 slice. The times are simulated.
256 devices in a mesh: pipe: 2 (over core), slab: 8 (over x, z_hi), dp: 16 (over z_lo, y).
Axes of the slice: x: 4, y: 4, z: 8 (z_hi: 2, z_lo: 4; z = z_hi * 4 + z_lo), core: 2. Of those that a mesh axis runs over, the one named last changes fastest.
Arguments:
- saved_inputs: bfloat16 [2, 2, 16, 2, 16, 16, 512], P('pipe', None, 'dp', None, 'slab'), may hold values from -12 to 12
- loss_cotangent: bfloat16 [2, 16, 2, 16, 16, 512], P(None, 'dp', None, 'slab'), may hold values from -3 to 3
- upstream: bfloat16 [16, 2, 16, 16, 512], P('dp', None, 'slab'), may hold values from -3 to 3
- conv_weight: bfloat16 [2, 512, 13824], P('pipe', 'dp'), may hold values from -0.0546875 to 0.0546875
- adagn_table: bfloat16 [2, 1000, 1024], P('pipe'), may hold values from -3 to 3
- timesteps: int32 [3, 16], P(None, 'dp'), may hold values from 0 to 999
- frame_counts: int32 [3, 16], P(None, 'dp'), may hold values from 1 to 2
Outputs:
- input_grads: bfloat16 [2, 2, 16, 2, 16, 16, 512], P('pipe', None, 'dp', None, 'slab')
- weight_grad: float32 [2, 512, 13824], P('pipe', 'dp')
- embed_grad: float32 [2, 2, 16, 1024], P('pipe', None, 'dp')
All inputs are finite; a program needn't handle non-finite values.
Results may differ from a plain program's by a relative error of at most 0.015.
Values may be sent and summed in bfloat16 or wider, within the bound.
A program may use at most 128 MiB of HBM per device.

v0:
```python
import math
import jax
import jax.numpy as jnp
from jax import lax
from jax.sharding import PartitionSpec as P

GROUPS = 32
EPS = 1e-05


def silu_grad(preact):
    sigma = jax.nn.sigmoid(preact)
    return sigma * (1.0 + preact * (1.0 - sigma))


def chunk_group_sums(values, groups_here):
    summed = jnp.sum(values.reshape(-1, values.shape[-1]), axis=0)
    return jnp.sum(summed.reshape(groups_here, -1), axis=1)


def tap_stack(padded, frames, rows, cells_wide):
    slices = []
    for depth_at in range(3):
        for vertical in range(3):
            for across in range(3):
                slices.append(
                    padded[
                        ...,
                        depth_at : depth_at + frames,
                        vertical : vertical + rows,
                        across : across + cells_wide,
                        :,
                    ]
                )
    return jnp.stack(slices, 0)


def local(
    saved_inputs, loss_cotangent, upstream, conv_weight, adagn_table, timesteps, frame_counts
):
    section_index = lax.axis_index("pipe")
    slab_index = lax.axis_index("slab")
    slab_count = lax.axis_size("slab")
    replicas = lax.axis_size("dp")
    inputs = saved_inputs[0, :, 0]
    tick_count, frames, slab_rows, cells_wide, channels = inputs.shape
    height_total = slab_rows * slab_count
    chunk = channels // slab_count
    per_group = channels // GROUPS
    groups_here = chunk // per_group
    step_table = adagn_table[0]
    taps = 27
    weight_local = conv_weight[0].reshape(-1, taps, channels)
    steps_now = lax.dynamic_slice_in_dim(timesteps[:, 0], section_index, tick_count)
    counts_now = lax.dynamic_slice_in_dim(frame_counts[:, 0], section_index, tick_count)
    chunk_start = slab_index * chunk
    weight_cols = lax.dynamic_slice_in_dim(weight_local, chunk_start, chunk, axis=2)
    weight_chunk = lax.all_gather(weight_cols, "dp", axis=0, tiled=True)
    kernel = weight_chunk.reshape(channels, 3, 3, 3, chunk)[:, ::-1, ::-1, ::-1, :]
    kernel = jnp.transpose(kernel, (1, 2, 3, 0, 4))
    inputs_chunk = lax.all_to_all(inputs, "slab", 4, 2, tiled=True)
    weight_norm = 1.0 / math.sqrt(tick_count * replicas * frames * height_total * cells_wide)
    embed_norm = 1.0 / math.sqrt(frames * height_total * cells_wide)

    def full_rows(rows_value):
        return lax.all_gather(rows_value, "slab", axis=1, tiled=True)

    cot_first = jnp.where(section_index == 1, loss_cotangent[0, 0], upstream[0])
    cot_full_first = full_rows(cot_first)
    cot_full_later = full_rows(loss_cotangent[1, 0])
    dx_list = []
    embed_list = []
    hidden_list = []
    cot_list = []
    cot_full = cot_full_first
    for tick_index in range(tick_count):
        steps = steps_now[tick_index]
        count = counts_now[tick_index]
        embedded = lax.dynamic_index_in_dim(step_table, steps, keepdims=False).astype(jnp.float32)
        gain = 1.0 + lax.dynamic_slice_in_dim(embedded, chunk_start, chunk)
        bias = lax.dynamic_slice_in_dim(embedded, channels + chunk_start, chunk)
        mask = (jnp.arange(frames, dtype=jnp.int32) < count).astype(jnp.float32)
        mask_cells = mask[:, None, None, None]
        valid = count.astype(jnp.float32) * float(height_total * cells_wide * per_group)
        values = inputs_chunk[tick_index].astype(jnp.float32)
        masked = values * mask_cells
        mean_g = chunk_group_sums(masked, groups_here) / valid
        var_g = chunk_group_sums(masked * values, groups_here) / valid - mean_g * mean_g
        rstd_g = lax.rsqrt(var_g + EPS)
        mean_c = jnp.repeat(mean_g, per_group)
        rstd_c = jnp.repeat(rstd_g, per_group)
        normed = (values - mean_c) * rstd_c
        preact = normed * gain + bias
        hidden = (jax.nn.silu(preact) * mask_cells).astype(jnp.bfloat16)
        hidden_list.append(hidden)
        upward = lax.conv_general_dilated(
            cot_full[None],
            kernel,
            window_strides=(1, 1, 1),
            padding=((1, 1), (1, 1), (1, 1)),
            dimension_numbers=("NDHWC", "DHWIO", "NDHWC"),
            preferred_element_type=jnp.float32,
        )[0]
        pre_grad = upward * silu_grad(preact) * mask_cells
        dnormed = pre_grad * gain
        sum_a = chunk_group_sums(dnormed, groups_here) / valid
        sum_b = chunk_group_sums(dnormed * normed, groups_here) / valid
        scale_part = jnp.sum(pre_grad * normed, axis=(0, 1, 2))
        shift_part = jnp.sum(pre_grad, axis=(0, 1, 2))
        branch = (
            rstd_c
            * (dnormed - jnp.repeat(sum_a, per_group) - normed * jnp.repeat(sum_b, per_group))
            * mask_cells
        )
        cot_chunk = lax.dynamic_slice_in_dim(cot_full, chunk_start, chunk, axis=3)
        result = (cot_chunk.astype(jnp.float32) + branch).astype(jnp.bfloat16)
        result_full = lax.all_gather(result, "slab", axis=3, tiled=True)
        dx_list.append(
            lax.dynamic_slice_in_dim(result_full, slab_index * slab_rows, slab_rows, axis=1)
        )
        embed_list.append(jnp.stack([scale_part, shift_part]))
        cot_list.append(cot_full)
        if tick_index + 1 < tick_count:
            received = lax.ppermute(result_full, "pipe", [(1, 0)])
            cot_full = jnp.where(section_index == 1, cot_full_later, received)
    embed_all = lax.all_gather(jnp.stack(embed_list), "slab", axis=2, tiled=True)
    embed_grad = embed_all.reshape(tick_count, 2 * channels) * embed_norm
    cot_all = jnp.stack(cot_list)
    hidden_all = jnp.pad(jnp.stack(hidden_list), ((0, 0), (1, 1), (1, 1), (1, 1), (0, 0)))
    hidden_taps = tap_stack(hidden_all, frames, height_total, cells_wide)
    grad_term = jnp.einsum(
        "kfrwo,tkfrwi->oti", cot_all, hidden_taps, preferred_element_type=jnp.float32
    )
    grad_shard = lax.psum_scatter(
        (grad_term * weight_norm).astype(jnp.bfloat16), "dp", scatter_dimension=0, tiled=True
    ).astype(jnp.float32)
    weight_grad = lax.all_gather(grad_shard, "slab", axis=2, tiled=True)
    weight_grad = weight_grad.reshape(weight_grad.shape[0], taps * channels)
    input_grads = jnp.stack(dx_list)[None, :, None]
    return (input_grads, weight_grad[None], embed_grad[None, :, None])


def solution(mesh):
    placed = (
        P("pipe", None, "dp", None, "slab", None, None),
        P(None, "dp", None, "slab", None, None),
        P("dp", None, "slab", None, None),
        P("pipe", "dp", None),
        P("pipe", None, None),
        P(None, "dp"),
        P(None, "dp"),
    )
    return jax.shard_map(
        local,
        mesh=mesh,
        in_specs=placed,
        out_specs=(
            P("pipe", None, "dp", None, "slab", None, None),
            P("pipe", "dp", None),
            P("pipe", None, "dp", None),
        ),
        check_vma=False,
    )
```

profile of v0, /device:TPU:40, one launch (start us, length us, event | category | flops | bytes accessed | tf_op | source)
XLA Modules:
  0.0 773.6 jit_solution(17184056033001340081)
XLA Ops:
  7.3 1.7 reshape_squeeze.3
  8.9 0.1 constant_dynamic-slice_fusion.6
  9.1 0.8 copy.161
  9.9 2.1 copy.156
  12.0 0.7 bitcast_bitcast_fusion
  12.7 1.7 reshape.434
  14.4 10.0 %all-to-all-start = ((bf16[8,2,4096]{2,1,0:T(2,128)(2,1)}), bf16[8,2,4096]{2,1,0:T(2,128)(2,1)S(1)}, u32[]{:S(2)}, u32[]{:S(2)}) async-start(bf16[8,2,4096]{2,1,0:T(2,128)(2,1)} %reshape.434), calls=%async_computation | async-start | bytes 262144 | tf_op jit(solution)/shard_map/all_to_all | solution.py:61
  24.6 0.7 fusion.112
  25.2 0.7 compare_convert_fusion
  25.9 0.6 fusion.111
  26.6 48.0 %all_gather.21 = bf16[2,16,16,512]{3,2,1,0:T(8,128)(2,1)S(1)} all-gather(bf16[2,2,16,512]{3,2,1,0:T(8,128)(2,1)S(1)} %bitcast_select_fusion.1), channel_id=1, replica_groups=mesh['pipe'=2,'slab'=8,'dp'=16] {'slab'}, dimensions={1}, use_global_device_ids=true | all-gather | bytes 589824 | tf_op jit(solution)/shard_map/all_gather | solution.py:66
  74.5 0.6 compare_convert_fusion.1
  78.9 0.3 copy.222
  79.3 0.4 copy.160
  79.7 0.1 slice.148
  81.1 0.8 dynamic-slice_convert_fusion.1
  81.9 0.7 reshape.435
  82.6 1.3 copy.157
  83.9 0.2 fusion.27
  84.3 0.1 reduce_sum.181
  84.4 0.1 reduce_sum.183
  84.9 17.5 %all-gather.4.cloned.1.call-done = bf16[512,27,64]{2,0,1:T(8,128)(2,1)} async-done(((bf16[32,27,64]{2,0,1:T(8,128)(2,1)}), bf16[512,27,64]{2,0,1:T(8,128)(2,1)}) %all-gather.4.cloned.1.call-update) | async-done | bytes 1769488 | tf_op jit(solution)/shard_map/all_gather | solution.py:58
  102.4 7.6 fusion.20
  110.2 0.2 multiply_reduce_fusion.3
  110.4 0.2 fusion.94
  110.8 0.1 reduce_sum.187
  111.1 0.1 reduce_sum.185
  111.4 0.1 add_convert_fusion.1
  111.6 0.8 copy.165
  112.3 156.0 %all_gather.23 = bf16[2,16,16,512]{2,1,0,3:T(8,128)(2,1)} all-gather(bf16[2,16,16,64]{2,1,0,3:T(8,128)(2,1)S(1)} %copy.165), channel_id=1, replica_groups=mesh['pipe'=2,'slab'=8,'dp'=16] {'slab'}, dimensions={3}, use_global_device_ids=true | all-gather | bytes 589824 | tf_op jit(solution)/shard_map/all_gather | solution.py:117
  268.3 4.4 copy.166
  272.7 1.3 collective-permute-start
  274.1 50.2 %all-gather = bf16[1,1,2,16,16,512]{5,4,3,2,1,0:T(8,128)(2,1)S(1)} all-gather(bf16[1,1,2,2,16,512]{5,4,3,2,1,0:T(8,128)(2,1)S(1)} %slice-done), channel_id=2, replica_groups=mesh['pipe'=2,'slab'=8,'dp'=16] {'slab'}, dimensions={3}, use_global_device_ids=true | all-gather | bytes 589824 | tf_op jit(solution)/shard_map/all_gather | solution.py:66
  324.3 0.1 reduce_sum.189
  324.6 0.1 reduce_sum.191
  325.1 0.3 copy.223
  325.5 0.4 copy.170
  325.9 0.1 slice.151
  326.0 7.6 fusion.17
  333.8 0.2 fusion.93
  334.7 0.1 fusion.47
  335.0 0.1 fusion.53
  335.2 0.1 fusion.55
  335.3 0.1 fusion.57
  336.3 5.7 fusion
  341.9 0.3 all-gather.6.cloned.1.call-start
  342.3 85.7 %reduce-scatter.2.cloned.1.call-done = bf16[32,27,64]{2,0,1:T(8,128)(2,1)} async-done(((bf16[512,27,64]{2,0,1:T(8,128)(2,1)}), bf16[32,27,64]{2,0,1:T(8,128)(2,1)}) %reduce-scatter.2.cloned.1.call-update) | async-done | bytes 110608 | tf_op jit(solution)/shard_map/reduce_scatter | solution.py:134
  428.0 2.7 copy.209
  430.9 0.1 reduce_sum.195
  431.3 0.1 reduce_sum.193
  431.6 0.2 multiply_reduce_fusion.2
  431.8 0.1 add_convert_fusion
  431.9 0.8 copy.179
  432.7 184.7 %all_gather.25 = bf16[2,16,16,512]{2,1,0,3:T(8,128)(2,1)S(1)} all-gather(bf16[2,16,16,64]{2,1,0,3:T(8,128)(2,1)S(1)} %copy.179), channel_id=1, replica_groups=mesh['pipe'=2,'slab'=8,'dp'=16] {'slab'}, dimensions={3}, use_global_device_ids=true | all-gather | bytes 589824 | tf_op jit(solution)/shard_map/all_gather | solution.py:117
  617.4 0.5 constant_dynamic-slice_fusion
  618.0 0.7 copy.221
  618.6 0.1 copy.211
  618.8 67.8 %all_gather.27 = f32[2,2,512]{1,0,2:T(2,128)S(1)} all-gather(f32[2,2,64]{1,0,2:T(2,128)S(1)} %copy.211), channel_id=1, replica_groups=mesh['pipe'=2,'slab'=8,'dp'=16] {'slab'}, dimensions={2}, use_global_device_ids=true | all-gather | bytes 9216 | tf_op jit(solution)/shard_map/all_gather | solution.py:126
  686.5 0.2 copy.212
  686.7 0.6 mul.507
  687.4 0.7 maximum_bitcast_fusion.1
  688.0 72.2 %all-gather.6.cloned.1.call-done = f32[32,27,512]{1,0,2:T(8,128)} async-done(((f32[32,27,64]{1,0,2:T(8,128)}), f32[32,27,512]{1,0,2:T(8,128)}) %all-gather.6.cloned.1.call-update) | async-done | bytes 1769488 | tf_op jit(solution)/shard_map/all_gather | solution.py:137
  760.3 5.3 copy.210
  765.5 1.6 broadcast_in_dim_reshape.2
  (92 shorter events, 4.8 us)
Async XLA Ops:
  7.2 17.3 %copy-start.2 = (s32[3,1]{0,1:T(1,128)S(1)}, s32[3,1]{0,1:T(1,128)}, u32[]{:S(2)}) copy-start(s32[3,1]{0,1:T(1,128)} %param.12) | copy-start | bytes 40
  7.2 17.3 %copy-start.3 = (s32[3,1]{0,1:T(1,128)S(1)}, s32[3,1]{0,1:T(1,128)}, u32[]{:S(2)}) copy-start(s32[3,1]{0,1:T(1,128)} %param.13) | copy-start | bytes 40
  7.2 19.4 %copy-start.1 = (bf16[1,2,2,16,512]{4,3,2,1,0:T(8,128)(2,1)S(1)}, bf16[1,2,2,16,512]{4,3,2,1,0:T(8,128)(2,1)}, u32[]{:S(2)}) copy-start(bf16[1,2,2,16,512]{4,3,2,1,0:T(8,128)(2,1)} %param.9) | copy-start | bytes 196612
  7.2 19.4 %copy-start = (bf16[2,1,2,2,16,512]{5,4,3,2,1,0:T(8,128)(2,1)S(1)}, bf16[2,1,2,2,16,512]{5,4,3,2,1,0:T(8,128)(2,1)}, u32[]{:S(2)}) copy-start(bf16[2,1,2,2,16,512]{5,4,3,2,1,0:T(8,128)(2,1)} %param.8) | copy-start | bytes 393220
  7.2 95.2 %all-gather.4.cloned.1.call-start = ((), (), s32[]{:S(2)}) async-start(), calls=%async_computation.2 | async-start | bytes 3760128 | tf_op jit(solution)/shard_map/all_gather | solution.py:58
  9.9 92.5 %copy-start.4 = (pred[8,3]{0,1:T(4,128)(4,1)S(1)}, pred[8,3]{0,1:T(4,128)(4,1)}, u32[]{:S(2)}) copy-start(pred[8,3]{0,1:T(4,128)(4,1)} %constant.79) | copy-start | bytes 76
  14.4 67.5 %all-to-all-start = ((bf16[8,2,4096]{2,1,0:T(2,128)(2,1)}), bf16[8,2,4096]{2,1,0:T(2,128)(2,1)S(1)}, u32[]{:S(2)}, u32[]{:S(2)}) async-start(bf16[8,2,4096]{2,1,0:T(2,128)(2,1)} %reshape.434), calls=%async_computation | async-start | bytes 262144 | tf_op jit(solution)/shard_map/all_to_all | solution.py:61
  24.4 403.6 %reduce-scatter.2.cloned.1.call-start = ((), (), s32[]{:S(2)}) async-start(), calls=%async_computation.3 | async-start | bytes 3760128 | tf_op jit(solution)/shard_map/reduce_scatter | solution.py:134
  110.0 164.1 %slice-start = ((bf16[2,1,2,2,16,512]{5,4,3,2,1,0:T(8,128)(2,1)}), bf16[1,1,2,2,16,512]{5,4,3,2,1,0:T(8,128)(2,1)S(1)}, s32[]{:S(2)}) async-start(bf16[2,1,2,2,16,512]{5,4,3,2,1,0:T(8,128)(2,1)} %param.8), calls=%async_computation.5 | async-start | bytes 131072 | tf_op jit(solution)/shard_map/slice | solution.py:70
  272.7 52.3 %collective-permute-start = (bf16[2,16,16,512]{3,2,1,0:T(8,128)(2,1)S(1)}, bf16[2,16,16,512]{3,2,1,0:T(8,128)(2,1)S(1)}, u32[]{:S(2)}, u32[]{:S(2)}) collective-permute-start(bf16[2,16,16,512]{3,2,1,0:T(8,128)(2,1)S(1)} %copy.166), channel_id=1, source_target_pairs={{128,0},{129,1},{130,2},{131,3},{132,4},{133,5},{134,6},{135,7},{1... | collective-permute-start | bytes 1572872 | tf_op jit(solution)/shard_map/ppermute | solution.py:124
  341.9 418.3 %all-gather.6.cloned.1.call-start = ((), (), s32[]{:S(2)}) async-start(), calls=%async_computation.4 | async-start | bytes 9437184 | tf_op jit(solution)/shard_map/all_gather | solution.py:137
Sparse Core Ops, SparseCore 0:
  10.4 91.9 all-gather.3
  342.1 85.8 reduce-scatter.1
  431.2 329.0 all-gather.5
where the time goes:
time: 774 us
  blocking collectives  507 us (66%)
  waiting for transfers between devices  175 us (23%)
  local copies, waits for them, and re-layouts  34.1 us (4%)
  matrix products  20.9 us (3%)
  between operations  19.2 us (2%)
  starting transfers between devices  11.7 us (2%)
    all_gather x2, blocking collectives, local(): result_full = lax.all_gather(result, 'slab', axis=3, tiled=True)  341 us
    all_gather x2, blocking collectives, full_rows(): return lax.all_gather(rows_value, 'slab', axis=1, tiled=True)  98.1 us
    reduce_scatter x1, waiting for transfers between devices, local(): lax.psum_scatter((grad_term * weight_norm).astype(jnp.bfloat16), 'dp', sc...  85.7 us
    all_gather x1, waiting for transfers between devices, local(): weight_grad = lax.all_gather(grad_shard, 'slab', axis=2, tiled=True)  72.2 us
    all_gather x1, blocking collectives, local(): lax.all_gather(jnp.stack(embed_list), 'slab', axis=2, tiled=True)  67.8 us
    all_gather x1, waiting for transfers between devices, local(): weight_chunk = lax.all_gather(weight_cols, 'dp', axis=0, tiled=True)  17.5 us
  transfers between devices with their start and end apart: 5, of which 3 were waited for; matrix products, arithmetic and copies ran while one was open for 2% of the time, Pallas kernels for 0%

commit v1 on v0

--- a/solution.py
+++ b/solution.py
@@ -3,6 +3,7 @@
 import jax.numpy as jnp
 from jax import lax
 from jax.sharding import PartitionSpec as P
+from jax.lax import all_to_all, axis_size
 
 GROUPS = 32
 EPS = 1e-05
@@ -134,7 +135,15 @@
     grad_shard = lax.psum_scatter(
         (grad_term * weight_norm).astype(jnp.bfloat16), "dp", scatter_dimension=0, tiled=True
     ).astype(jnp.float32)
-    weight_grad = lax.all_gather(grad_shard, "slab", axis=2, tiled=True)
+    weight_grad = jnp.concatenate(
+        all_to_all(
+            jnp.stack([grad_shard for _ in range(axis_size("slab"))], axis=0),
+            "slab",
+            split_axis=0,
+            concat_axis=0,
+        ),
+        axis=2,
+    )
     weight_grad = weight_grad.reshape(weight_grad.shape[0], taps * channels)
     input_grads = jnp.stack(dx_list)[None, :, None]
     return (input_grads, weight_grad[None], embed_grad[None, :, None])

time: 774 us -> 714 us (0.922)
  the two profiles are of different devices: /device:TPU:40 before, /device:TPU:24 now
where the time goes in v1:
time: 714 us; the launch traced here: 710 us
  blocking collectives  495 us (69%)
  waiting for transfers between devices  97 us (14%)
  local copies, waits for them, and re-layouts  38.6 us (5%)
  starting transfers between devices  21.4 us (3%)
  matrix products  20.9 us (3%)
  between operations  19.7 us (3%)
  other arithmetic  17.4 us (2%)
    all_gather x2, blocking collectives, local(): result_full = lax.all_gather(result, 'slab', axis=3, tiled=True)  348 us
    all_gather x2, blocking collectives, full_rows(): return lax.all_gather(rows_value, 'slab', axis=1, tiled=True)  99.7 us
    reduce_scatter x1, waiting for transfers between devices, local(): lax.psum_scatter((grad_term * weight_norm).astype(jnp.bfloat16), 'dp', sc...  82.9 us
    all_gather x1, blocking collectives, local(): lax.all_gather(jnp.stack(embed_list), 'slab', axis=2, tiled=True)  46.8 us
    unnamed x55, local copies, waits for them, and re-layouts  16.8 us
    conv_general_dilated x2, matrix products, local(): lax.conv_general_dilated(cot_full[None], kernel, window_strides=(1, 1, 1)...  15.3 us
  transfers between devices with their start and end apart: 5, of which 2 were waited for; matrix products, arithmetic and copies ran while one was open for 3% of the time, Pallas kernels for 0%

profile of v1, /device:TPU:24, one launch (start us, length us, event | category | flops | bytes accessed | tf_op | source)
XLA Modules:
  0.0 709.7 jit_solution(3732292362774109675)
XLA Ops:
  7.3 1.7 reshape_squeeze.3
  8.9 0.1 constant_dynamic-slice_fusion.6
  9.1 0.8 copy.219
  9.9 2.1 copy.214
  12.0 0.7 bitcast_bitcast_fusion.1
  12.7 1.7 reshape.440
  14.4 10.9 %all-to-all-start = ((bf16[8,2,4096]{2,1,0:T(2,128)(2,1)}), bf16[8,2,4096]{2,1,0:T(2,128)(2,1)S(1)}, u32[]{:S(2)}, u32[]{:S(2)}) async-start(bf16[8,2,4096]{2,1,0:T(2,128)(2,1)} %reshape.440), calls=%async_computation | async-start | bytes 262144 | tf_op jit(solution)/shard_map/all_to_all | solution.py:62
  25.5 0.7 fusion.112
  26.1 0.7 compare_convert_fusion
  26.8 0.6 fusion.111
  27.5 51.7 %all_gather.18 = bf16[2,16,16,512]{3,2,1,0:T(8,128)(2,1)S(1)} all-gather(bf16[2,2,16,512]{3,2,1,0:T(8,128)(2,1)S(1)} %bitcast_select_fusion.1), channel_id=1, replica_groups=mesh['pipe'=2,'slab'=8,'dp'=16] {'slab'}, dimensions={1}, use_global_device_ids=true | all-gather | bytes 589824 | tf_op jit(solution)/shard_map/all_gather | solution.py:67
  79.2 0.6 compare_convert_fusion.1
  83.6 0.3 copy.279
  84.0 0.4 copy.218
  84.4 0.1 slice.148
  85.7 0.8 dynamic-slice_convert_fusion.1
  86.6 0.7 reshape.441
  87.3 1.3 copy.215
  88.6 0.2 fusion.27
  89.6 14.1 %all-gather.3.cloned.1.call-done = bf16[512,27,64]{2,0,1:T(8,128)(2,1)} async-done(((bf16[32,27,64]{2,0,1:T(8,128)(2,1)}), bf16[512,27,64]{2,0,1:T(8,128)(2,1)}) %all-gather.3.cloned.1.call-update) | async-done | bytes 1769488 | tf_op jit(solution)/shard_map/all_gather | solution.py:59
  103.7 7.6 %fusion.20 = f32[2,16,8,3,64]{4,2,3,1,0:T(8,128)S(1)} fusion(bf16[512,3,3,3,64]{4,0,3,2,1:T(8,128)(2,1)} %bitcast.342, bf16[2,16,1,7,2,512]{5,3,4,1,0,2:T(8,128)(2,1)S(1)} %slice.148, bf16[2,16,1,8,3,512]{5,3,4,1,0,2:T(8,128)(2,1)S(1)} %copy.218, pred[8,3]{0,1:T(4,128)(4,1)S(1)} %copy-done.9), kind=kOutput, calls=%fused_computation.44 | convolution fusion | flops 872202240 | bytes 3211288 | tf_op jit(solution)/shard_map/conv_general_dilated | solution.py:97
  111.4 0.8 multiply_reduce_fusion.3
  112.2 0.2 fusion.94
  112.6 0.1 reduce_sum.187
  113.0 0.1 reduce_sum.185
  113.3 0.1 add_convert_fusion.1
  113.4 0.8 copy.223
  114.2 160.9 %all_gather.20 = bf16[2,16,16,512]{2,1,0,3:T(8,128)(2,1)} all-gather(bf16[2,16,16,64]{2,1,0,3:T(8,128)(2,1)S(1)} %copy.223), channel_id=1, replica_groups=mesh['pipe'=2,'slab'=8,'dp'=16] {'slab'}, dimensions={3}, use_global_device_ids=true | all-gather | bytes 589824 | tf_op jit(solution)/shard_map/all_gather | solution.py:118
  275.1 4.4 copy.224
  279.5 1.3 collective-permute-start
  280.9 47.9 %all-gather = bf16[1,1,2,16,16,512]{5,4,3,2,1,0:T(8,128)(2,1)S(1)} all-gather(bf16[1,1,2,2,16,512]{5,4,3,2,1,0:T(8,128)(2,1)S(1)} %slice-done), channel_id=2, replica_groups=mesh['pipe'=2,'slab'=8,'dp'=16] {'slab'}, dimensions={3}, use_global_device_ids=true | all-gather | bytes 589824 | tf_op jit(solution)/shard_map/all_gather | solution.py:67
  328.9 0.1 reduce_sum.189
  329.1 0.1 reduce_sum.191
  329.7 0.3 copy.280
  330.1 0.4 copy.228
  330.5 0.1 slice.151
  330.6 7.6 %fusion.17 = f32[2,16,8,3,64]{4,2,3,1,0:T(8,128)S(1)} fusion(bf16[512,3,3,3,64]{4,0,3,2,1:T(8,128)(2,1)} %bitcast.343, bf16[2,16,1,7,2,512]{5,3,4,1,0,2:T(8,128)(2,1)S(1)} %slice.151, bf16[2,16,1,8,3,512]{5,3,4,1,0,2:T(8,128)(2,1)S(1)} %copy.228, pred[8,3]{0,1:T(4,128)(4,1)S(1)} %copy-done.9), kind=kOutput, calls=%fused_computation.43 | convolution fusion | flops 872202240 | bytes 3211288 | tf_op jit(solution)/shard_map/conv_general_dilated | solution.py:97
  338.4 0.9 fusion.93
  341.6 5.7 fusion
  347.3 82.9 %reduce-scatter.2.cloned.1.call-done = bf16[32,27,64]{2,0,1:T(8,128)(2,1)} async-done(((bf16[512,27,64]{2,0,1:T(8,128)(2,1)}), bf16[32,27,64]{2,0,1:T(8,128)(2,1)}) %reduce-scatter.2.cloned.1.call-update) | async-done | bytes 110608 | tf_op jit(solution)/shard_map/reduce_scatter | solution.py:135
  430.2 1.4 broadcast_bitcast_fusion
  431.6 4.1 reshape.442
  435.7 9.1 %all-to-all-start.1 = ((f32[8,1,55296]{2,1,0:T(1,128)}), f32[8,1,55296]{2,1,0:T(1,128)S(1)}, u32[]{:S(2)}, u32[]{:S(2)}) async-start(f32[8,1,55296]{2,1,0:T(1,128)} %reshape.442), calls=%async_computation.2 | async-start | bytes 3538944 | tf_op jit(solution)/shard_map/all_to_all | solution.py:139
  444.8 0.7 maximum_bitcast_fusion.2
  445.4 0.8 dynamic-slice_bitcast_fusion
  446.3 1.1 fusion.107
  447.5 0.1 reduce_sum.195
  447.8 0.1 reduce_sum.193
  448.1 1.3 multiply_reduce_fusion.2
  449.4 1.1 add_convert_fusion
  450.5 0.8 copy.237
  451.3 187.4 %all_gather.22 = bf16[2,16,16,512]{2,1,0,3:T(8,128)(2,1)S(1)} all-gather(bf16[2,16,16,64]{2,1,0,3:T(8,128)(2,1)S(1)} %copy.237), channel_id=1, replica_groups=mesh['pipe'=2,'slab'=8,'dp'=16] {'slab'}, dimensions={3}, use_global_device_ids=true | all-gather | bytes 589824 | tf_op jit(solution)/shard_map/all_gather | solution.py:118
  638.7 0.5 constant_dynamic-slice_fusion
  639.3 0.7 copy.278
  640.1 46.8 %all_gather.23 = f32[2,2,512]{1,0,2:T(2,128)S(1)} all-gather(f32[2,2,64]{1,0,2:T(2,128)S(1)} %copy.268), channel_id=1, replica_groups=mesh['pipe'=2,'slab'=8,'dp'=16] {'slab'}, dimensions={2}, use_global_device_ids=true | all-gather | bytes 9216 | tf_op jit(solution)/shard_map/all_gather | solution.py:127
  686.8 0.2 copy.269
  687.0 0.6 mul.507
  687.7 0.7 maximum_bitcast_fusion.1
  688.3 0.6 broadcast.462
  688.9 6.6 reduce.8
  695.6 2.9 reshape.443
  698.4 0.4 bitcast_bitcast_fusion
  698.8 2.1 copy.267
  700.9 1.8 broadcast_in_dim_reshape_reshape.3
  (106 shorter events, 5.5 us)
Async XLA Ops:
  7.2 18.2 %copy-start.7 = (s32[3,1]{0,1:T(1,128)S(1)}, s32[3,1]{0,1:T(1,128)}, u32[]{:S(2)}) copy-start(s32[3,1]{0,1:T(1,128)} %param.12) | copy-start | bytes 40
  7.2 18.2 %copy-start.8 = (s32[3,1]{0,1:T(1,128)S(1)}, s32[3,1]{0,1:T(1,128)}, u32[]{:S(2)}) copy-start(s32[3,1]{0,1:T(1,128)} %param.13) | copy-start | bytes 40
  7.2 20.3 %copy-start.5 = (bf16[1,2,2,16,512]{4,3,2,1,0:T(8,128)(2,1)S(1)}, bf16[1,2,2,16,512]{4,3,2,1,0:T(8,128)(2,1)}, u32[]{:S(2)}) copy-start(bf16[1,2,2,16,512]{4,3,2,1,0:T(8,128)(2,1)} %param.9) | copy-start | bytes 196612
  7.2 20.3 %copy-start.4 = (bf16[2,1,2,2,16,512]{5,4,3,2,1,0:T(8,128)(2,1)S(1)}, bf16[2,1,2,2,16,512]{5,4,3,2,1,0:T(8,128)(2,1)}, u32[]{:S(2)}) copy-start(bf16[2,1,2,2,16,512]{5,4,3,2,1,0:T(8,128)(2,1)} %param.8) | copy-start | bytes 393220
  7.2 96.5 %all-gather.3.cloned.1.call-start = ((), (), s32[]{:S(2)}) async-start(), calls=%async_computation.3 | async-start | bytes 3760128 | tf_op jit(solution)/shard_map/all_gather | solution.py:59
  9.9 93.8 %copy-start.9 = (pred[8,3]{0,1:T(4,128)(4,1)S(1)}, pred[8,3]{0,1:T(4,128)(4,1)}, u32[]{:S(2)}) copy-start(pred[8,3]{0,1:T(4,128)(4,1)} %constant.79) | copy-start | bytes 76
  14.4 72.2 %all-to-all-start = ((bf16[8,2,4096]{2,1,0:T(2,128)(2,1)}), bf16[8,2,4096]{2,1,0:T(2,128)(2,1)S(1)}, u32[]{:S(2)}, u32[]{:S(2)}) async-start(bf16[8,2,4096]{2,1,0:T(2,128)(2,1)} %reshape.440), calls=%async_computation | async-start | bytes 262144 | tf_op jit(solution)/shard_map/all_to_all | solution.py:62
  25.3 404.9 %reduce-scatter.2.cloned.1.call-start = ((), (), s32[]{:S(2)}) async-start(), calls=%async_computation.4 | async-start | bytes 3760128 | tf_op jit(solution)/shard_map/reduce_scatter | solution.py:135
  89.6 248.8 %copy-start = (f32[1,2,8,2,16,64]{5,4,3,2,1,0:T(8,128)}, f32[1,2,8,2,16,64]{5,4,3,2,1,0:T(8,128)S(1)}, u32[]{:S(2)}) copy-start(f32[1,2,8,2,16,64]{5,4,3,2,1,0:T(8,128)S(1)} %get-tuple-element.45) | copy-start | bytes 393220
  111.3 169.6 %slice-start = ((bf16[2,1,2,2,16,512]{5,4,3,2,1,0:T(8,128)(2,1)}), bf16[1,1,2,2,16,512]{5,4,3,2,1,0:T(8,128)(2,1)S(1)}, s32[]{:S(2)}) async-start(bf16[2,1,2,2,16,512]{5,4,3,2,1,0:T(8,128)(2,1)} %param.8), calls=%async_computation.5 | async-start | bytes 131072 | tf_op jit(solution)/shard_map/slice | solution.py:71
  279.5 50.1 %copy-start.3 = (bf16[2,16,16,512]{3,2,1,0:T(8,128)(2,1)}, bf16[2,16,16,512]{3,2,1,0:T(8,128)(2,1)S(1)}, u32[]{:S(2)}) copy-start(bf16[2,16,16,512]{3,2,1,0:T(8,128)(2,1)S(1)} %copy.224) | copy-start | bytes 1572868
  279.5 50.1 %collective-permute-start = (bf16[2,16,16,512]{3,2,1,0:T(8,128)(2,1)S(1)}, bf16[2,16,16,512]{3,2,1,0:T(8,128)(2,1)S(1)}, u32[]{:S(2)}, u32[]{:S(2)}) collective-permute-start(bf16[2,16,16,512]{3,2,1,0:T(8,128)(2,1)S(1)} %copy.224), channel_id=1, source_target_pairs={{128,0},{129,1},{130,2},{131,3},{132,4},{133,5},{134,6},{135,7},{1... | collective-permute-start | bytes 1572872 | tf_op jit(solution)/shard_map/ppermute | solution.py:125
  280.9 57.5 %copy-start.6 = (f32[64]{0:T(128)}, f32[64]{0:T(128)S(1)}, u32[]{:S(2)}) copy-start(f32[64]{0:T(128)S(1)} %get-tuple-element.49) | copy-start | bytes 772
  329.7 11.9 %copy-start.1 = (bf16[2,16,16,512]{3,2,1,0:T(8,128)(2,1)}, bf16[2,16,16,512]{3,2,1,0:T(8,128)(2,1)S(1)}, u32[]{:S(2)}) copy-start(bf16[2,16,16,512]{3,2,1,0:T(8,128)(2,1)S(1)} %bitcast_select_fusion) | copy-start | bytes 1572868
  338.4 3.1 copy-start.2
  435.7 252.7 %all-to-all-start.1 = ((f32[8,1,55296]{2,1,0:T(1,128)}), f32[8,1,55296]{2,1,0:T(1,128)S(1)}, u32[]{:S(2)}, u32[]{:S(2)}) async-start(f32[8,1,55296]{2,1,0:T(1,128)} %reshape.442), calls=%async_computation.2 | async-start | bytes 3538944 | tf_op jit(solution)/shard_map/all_to_all | solution.py:139
Sparse Core Ops, SparseCore 0:
  10.4 93.2 all-gather.2
  347.4 82.7 reduce-scatter.1
